TPU v7x, 256 devices: a whole 4x4x8 slice. The times are simulated.
256 devices in a mesh: ctx: 32 (over y, x, core), tp: 8 (over z).
Axes of the slice: x: 4, y: 4, z: 8, core: 2. Of those that a mesh axis runs over, the one named last changes fastest.
Arguments:
- query_rows: bfloat16 [32768, 4096], P('ctx', 'tp'), may hold values from -6 to 6
- key_rows: bfloat16 [32768, 4096], P('ctx', 'tp'), may hold values from -6 to 6
- value_rows: bfloat16 [32768, 4096], P('ctx', 'tp'), may hold values from -6 to 6
- layer_grad: bfloat16 [32768, 4096], P('ctx', 'tp'), may hold values from -6 to 6
- out_weight: bfloat16 [4096, 4096], P('tp'), may hold values from -0.09375 to 0.09375
Outputs:
- query_grad: bfloat16 [32768, 4096], P('ctx', 'tp')
- key_grad: bfloat16 [32768, 4096], P('ctx', 'tp')
- value_grad: bfloat16 [32768, 4096], P('ctx', 'tp')
All inputs are finite; a program needn't handle non-finite values.
Results may differ from a plain program's by a relative error of at most 0.0058.
Values may be sent and summed in bfloat16 or wider, within the bound.
No kernel may reach another device: no remote copies, remote signals or barrier semaphores. Data moves between devices by JAX's collectives and lax.ppermute only.
A program may use at most 128 MiB of HBM per device.

v0:
```python
import jax
import jax.numpy as jnp
from jax import lax
from jax.sharding import Mesh
from jax.sharding import PartitionSpec as P

HEAD = 128
CTX = ("ctx_0", "ctx_1", "ctx_2")


def in_blocks(shard, dim, peers):
    lengths = shard.shape
    parts = shard.reshape(*lengths[:dim], peers, lengths[dim] // peers, *lengths[dim + 1 :])
    return jnp.moveaxis(parts, dim, 0)


def in_order(parts, dim):
    lengths = list(parts.shape[1:])
    lengths[dim] *= parts.shape[0]
    return jnp.moveaxis(parts, 0, dim).reshape(lengths)


def moved_by_axis(parts, axes, order):
    inside = parts.shape[1:]
    result = parts.reshape(*(lax.axis_size(a) for a in axes), *inside)
    for k in order:
        result = lax.all_to_all(result, axes[k], k, k, tiled=True)
    return result.reshape(-1, *inside)


def core_and_chips(shard, groups, order, split_dim, concat_dim):
    peers = lax.axis_size(groups[0]) * lax.axis_size(groups[1])
    parts = in_blocks(shard, split_dim, peers)
    return in_order(moved_by_axis(parts, groups, order), concat_dim)


def local(query_rows, key_rows, value_rows, layer_grad, out_weight):
    tokens = query_rows.shape[0]
    columns = query_rows.shape[1]
    head_count = columns // HEAD
    devices = lax.axis_size(CTX)
    factor = float((HEAD * tokens * devices) ** (-0.5))
    grad_heads = lax.dot_general(
        lax.all_gather(layer_grad, "tp", axis=1, tiled=True),
        out_weight,
        (((1,), (1,)), ((), ())),
        preferred_element_type=jnp.float32,
    ).astype(jnp.bfloat16)
    query_three = query_rows.reshape(tokens, head_count, HEAD)
    key_three = key_rows.reshape(tokens, head_count, HEAD)
    value_three = value_rows.reshape(tokens, head_count, HEAD)
    gradient_three = grad_heads.reshape(tokens, head_count, HEAD)
    key_value_here = jnp.einsum(
        "lbg,lbz->bgz", key_three, value_three, preferred_element_type=jnp.float32
    )
    gradient_here = jnp.einsum(
        "lbg,lbz->bgz", query_three, gradient_three, preferred_element_type=jnp.float32
    )
    state_shape = key_value_here.shape
    slice_len = key_value_here.size // devices
    kv_slices = key_value_here.reshape(devices, slice_len)
    grad_slices = gradient_here.reshape(devices, slice_len)
    kv_sources, grad_sources = (
        core_and_chips(kv_slices, (("ctx_0", "ctx_1"), "ctx_2"), (1, 0), 0, 0),
        core_and_chips(grad_slices, (("ctx_0", "ctx_1"), "ctx_2"), (1, 0), 0, 0),
    )
    zero_row = jnp.zeros((1, slice_len), jnp.float32)
    kv_prefix = jnp.concatenate([zero_row, jnp.cumsum(kv_sources, 0)[:-1]], 0)
    grad_suffix = jnp.cumsum(grad_sources[::-1], 0)[::-1]
    grad_suffix = jnp.concatenate([grad_suffix[1:], zero_row], 0)
    kv_mine, grad_mine = (
        core_and_chips(
            kv_prefix.astype(jnp.bfloat16), (("ctx_0", "ctx_1"), "ctx_2"), (1, 0), 0, 0
        ).astype(kv_prefix.dtype),
        core_and_chips(
            grad_suffix.astype(jnp.bfloat16), (("ctx_0", "ctx_1"), "ctx_2"), (1, 0), 0, 0
        ).astype(grad_suffix.dtype),
    )
    kv_before = kv_mine.reshape(state_shape)
    grad_after = grad_mine.reshape(state_shape)
    key_value_state = kv_before.astype(jnp.bfloat16)
    gradient_state = grad_after.astype(jnp.bfloat16)
    block_len = min(512, tokens)
    key_cols = jnp.arange(tokens)
    key_total = jnp.einsum(
        "yqr,qmr->yqm", value_three, gradient_state, preferred_element_type=jnp.float32
    )
    value_total = jnp.einsum(
        "jaq,aqd->jad", key_three, gradient_state, preferred_element_type=jnp.float32
    )
    query_parts = []
    for begin_row in range(0, tokens, block_len):
        query_blk = query_three[begin_row : begin_row + block_len]
        gradient_block = gradient_three[begin_row : begin_row + block_len]
        row_pos = begin_row + jnp.arange(block_len)
        causal = (row_pos[:, None] >= key_cols[None, :])[None]
        inside_gradient = jnp.einsum(
            "thv,shv->hts", gradient_block, value_three, preferred_element_type=jnp.float32
        )
        inside_gradient = jnp.where(causal, inside_gradient, jnp.float32(0.0)).astype(jnp.bfloat16)
        inside_query = jnp.einsum(
            "thk,shk->hts", query_blk, key_three, preferred_element_type=jnp.float32
        )
        inside_query = jnp.where(causal, inside_query, jnp.float32(0.0)).astype(jnp.bfloat16)
        query_part = jnp.einsum(
            "vmr,rve->mve", inside_gradient, key_three, preferred_element_type=jnp.float32
        )
        query_part = query_part + jnp.einsum(
            "nde,dze->ndz", gradient_block, key_value_state, preferred_element_type=jnp.float32
        )
        query_parts.append((factor * query_part).astype(jnp.bfloat16))
        key_total = key_total + jnp.einsum(
            "cxd,xcr->dcr", inside_gradient, query_blk, preferred_element_type=jnp.float32
        )
        value_total = value_total + jnp.einsum(
            "kzx,zkm->xkm", inside_query, gradient_block, preferred_element_type=jnp.float32
        )
    query_grad = jnp.concatenate(query_parts, 0).reshape(tokens, columns)
    key_grad = (factor * key_total).astype(jnp.bfloat16).reshape(tokens, columns)
    value_grad = (factor * value_total).astype(jnp.bfloat16).reshape(tokens, columns)
    return (query_grad, key_grad, value_grad)


def solution(mesh):
    finer = Mesh(mesh.devices.reshape(4, 4, 2, mesh.shape["tp"]), ("ctx_0", "ctx_1", "ctx_2", "tp"))
    return jax.shard_map(
        local,
        mesh=finer,
        in_specs=(P(CTX, "tp"), P(CTX, "tp"), P(CTX, "tp"), P(CTX, "tp"), P("tp", None)),
        out_specs=(P(CTX, "tp"), P(CTX, "tp"), P(CTX, "tp")),
        check_vma=False,
    )
```

profile of v0, /device:TPU:1, one launch (start us, length us, event | category | flops | bytes accessed | tf_op | source)
XLA Modules:
  0.0 205.4 jit_solution(13467134695923342138)
XLA Ops:
  10.4 6.8 %all_to_all.40 = f32[16,2,1,2048]{3,0,2,1:T(8,128)S(1)} all-to-all(f32[16,2,1,2048]{3,0,2,1:T(8,128)S(1)} %copy.56), channel_id=1, replica_groups=mesh['ctx_0'=4,'ctx_1'=4,'ctx_2'=2,'tp'=8] {'ctx_2'}, dimensions={1} | all-to-all | bytes 524288 | tf_op jit(solution)/shard_map/all_to_all | solution.py:27
  18.1 5.0 %all-to-all-start.1 = ((f32[16,2,1,2048]{3,1,2,0:T(2,128)}), f32[16,2,1,2048]{3,1,2,0:T(2,128)S(1)}, u32[]{:S(2)}, u32[]{:S(2)}) async-start(f32[16,2,1,2048]{3,1,2,0:T(2,128)} %copy.57), calls=%async_computation.1 | async-start | bytes 524288 | tf_op jit(solution)/shard_map/all_to_all | solution.py:27
  26.5 4.8 %all-to-all-done.1 = f32[16,2,1,2048]{3,1,2,0:T(2,128)S(1)} async-done(((f32[16,2,1,2048]{3,1,2,0:T(2,128)}), f32[16,2,1,2048]{3,1,2,0:T(2,128)S(1)}, u32[]{:S(2)}, u32[]{:S(2)}) %all-to-all-start.1) | async-done | bytes 262176 | tf_op jit(solution)/shard_map/all_to_all | solution.py:27
  31.9 5.0 %all_to_all.41 = bf16[16,2,1,2048]{3,0,2,1:T(8,128)(2,1)S(1)} all-to-all(bf16[16,2,1,2048]{3,0,2,1:T(8,128)(2,1)S(1)} %copy.58), channel_id=1, replica_groups=mesh['ctx_0'=4,'ctx_1'=4,'ctx_2'=2,'tp'=8] {'ctx_2'}, dimensions={1} | all-to-all | bytes 262144 | tf_op jit(solution)/shard_map/all_to_all | solution.py:27
  37.7 3.7 %all-to-all-start.3 = ((bf16[16,2,1,2048]{3,1,2,0:T(2,128)(2,1)}), bf16[16,2,1,2048]{3,1,2,0:T(2,128)(2,1)S(1)}, u32[]{:S(2)}, u32[]{:S(2)}) async-start(bf16[16,2,1,2048]{3,1,2,0:T(2,128)(2,1)} %copy.59), calls=%async_computation.3 | async-start | bytes 262144 | tf_op jit(solution)/shard_map/all_to_all | solution.py:27
  41.5 6.5 %all-to-all-done.3 = bf16[16,2,1,2048]{3,1,2,0:T(2,128)(2,1)S(1)} async-done(((bf16[16,2,1,2048]{3,1,2,0:T(2,128)(2,1)}), bf16[16,2,1,2048]{3,1,2,0:T(2,128)(2,1)S(1)}, u32[]{:S(2)}, u32[]{:S(2)}) %all-to-all-start.3) | async-done | bytes 131104 | tf_op jit(solution)/shard_map/all_to_all | solution.py:27
  48.1 59.4 %all-gather.2.cloned.1.call-done = bf16[1024,4096]{1,0:T(8,128)(2,1)} async-done(((bf16[1024,512]{1,0:T(8,128)(2,1)}), bf16[1024,4096]{1,0:T(8,128)(2,1)}) %all-gather.2.cloned.1.call-update) | async-done | bytes 8388624 | tf_op jit(solution)/shard_map/all_gather | solution.py:44
  107.5 9.1 %convolution_convert_fusion = bf16[1024,512]{0,1:T(8,128)(2,1)S(1)} fusion(bf16[1024,4096]{1,0:T(8,128)(2,1)} %all-gather.2.cloned.1.call-done, bf16[512,4096]{1,0:T(8,128)(2,1)} %param.9), kind=kOutput, calls=%fused_computation.19 | convolution fusion | flops 4295491584 | bytes 13631488 | tf_op jit(solution)/shard_map/dot_general | solution.py:43
  122.3 5.1 %fusion = f32[4,128,1024]{2,1,0:T(8,128)} fusion(bf16[512,4,128]{0,2,1:T(8,128)(2,1)} %bitcast.151, pred[512,1024]{1,0:T(8,128)(4,1)} %copy-done.10, bf16[512,4,128]{0,2,1:T(8,128)(2,1)} %bitcast.145, bf16[1024,512]{1,0:T(8,128)(2,1)} %param.6), kind=kOutput, calls=%fused_computation.4 | convolution fusion | flops 1077936128 | bytes 4718592 | tf_op jit(solution)/shard_map/kzx,zkm->xkm/dot_general | solution.py:115
  127.4 2.8 %select_convert_fusion.2 = bf16[4,512,1024]{2,1,0:T(8,128)(2,1)S(1)} fusion(pred[512,1024]{1,0:T(8,128)(4,1)} %iota_compare_fusion, bf16[512,4,128]{0,2,1:T(8,128)(2,1)} %bitcast.147, bf16[1024,512]{1,0:T(8,128)(2,1)S(1)} %copy-done), kind=kOutput, calls=%fused_computation.2 | convolution fusion | flops 541065216 | bytes 6291456 | tf_op jit(solution)/shard_map/thv,shv->hts/dot_general | solution.py:97
  138.8 4.4 %all_to_all.42 = f32[16,2,1,2048]{3,0,2,1:T(8,128)S(1)} all-to-all(f32[16,2,1,2048]{3,0,2,1:T(8,128)S(1)} %copy.70), channel_id=1, replica_groups=mesh['ctx_0'=4,'ctx_1'=4,'ctx_2'=2,'tp'=8] {'ctx_2'}, dimensions={1} | all-to-all | bytes 524288 | tf_op jit(solution)/shard_map/all_to_all | solution.py:27
  144.1 6.5 %all-to-all-start.5 = ((f32[16,2,1,2048]{3,1,2,0:T(2,128)}), f32[16,2,1,2048]{3,1,2,0:T(2,128)S(1)}, u32[]{:S(2)}, u32[]{:S(2)}) async-start(f32[16,2,1,2048]{3,1,2,0:T(2,128)} %copy.71), calls=%async_computation.5 | async-start | bytes 524288 | tf_op jit(solution)/shard_map/all_to_all | solution.py:27
  150.6 5.1 %fusion.1 = f32[4,128,1024]{2,1,0:T(8,128)} fusion(bf16[512,4,128]{0,2,1:T(8,128)(2,1)} %bitcast.148, pred[512,1024]{1,0:T(8,128)(4,1)} %iota_compare_fusion, bf16[512,4,128]{0,2,1:T(8,128)(2,1)} %bitcast.143, bf16[1024,512]{1,0:T(8,128)(2,1)} %param.6), kind=kOutput, calls=%fused_computation.5 | convolution fusion | flops 1077936128 | bytes 4718592 | tf_op jit(solution)/shard_map/kzx,zkm->xkm/dot_general | solution.py:115
  155.7 2.5 %fusion.16 = bf16[512,4,128]{2,0,1:T(8,128)(2,1)} fusion(f32[512,4,128]{2,0,1:T(8,128)} %convolution_bitcast_fusion.3, bf16[4,128,128]{2,1,0:T(8,128)(2,1)S(1)} %reshape_reshape.20, bf16[512,4,128]{0,2,1:T(8,128)(2,1)} %bitcast.152), kind=kOutput, calls=%fused_computation.28 | convolution fusion | flops 67895296 | bytes 2228224 | tf_op jit(solution)/shard_map/nde,dze->ndz/dot_general | solution.py:108
  158.3 2.5 %fusion.17 = bf16[512,4,128]{2,0,1:T(8,128)(2,1)} fusion(f32[512,4,128]{2,0,1:T(8,128)} %convolution_bitcast_fusion.1, bf16[4,128,128]{2,1,0:T(8,128)(2,1)S(1)} %reshape_reshape.20, bf16[512,4,128]{0,2,1:T(8,128)(2,1)} %bitcast.149), kind=kOutput, calls=%fused_computation.29 | convolution fusion | flops 67895296 | bytes 2228224 | tf_op jit(solution)/shard_map/nde,dze->ndz/dot_general | solution.py:108
  161.7 5.8 %rev.4 = f32[32,2048]{1,0:T(8,128)S(1)} reverse(f32[32,2048]{1,0:T(8,128)} %reshape_reshape.21), dimensions={0} | reverse | bytes 524288 | tf_op jit(solution)/shard_map/rev | solution.py:69
  168.4 4.1 %all_to_all.43 = bf16[16,2,1,2048]{3,0,2,1:T(8,128)(2,1)S(1)} all-to-all(bf16[16,2,1,2048]{3,0,2,1:T(8,128)(2,1)S(1)} %copy.72), channel_id=1, replica_groups=mesh['ctx_0'=4,'ctx_1'=4,'ctx_2'=2,'tp'=8] {'ctx_2'}, dimensions={1} | all-to-all | bytes 262144 | tf_op jit(solution)/shard_map/all_to_all | solution.py:27
  173.3 6.9 %all-to-all-start.7 = ((bf16[16,2,1,2048]{3,1,2,0:T(2,128)(2,1)}), bf16[16,2,1,2048]{3,1,2,0:T(2,128)(2,1)S(1)}, u32[]{:S(2)}, u32[]{:S(2)}) async-start(bf16[16,2,1,2048]{3,1,2,0:T(2,128)(2,1)} %copy.73), calls=%async_computation.7 | async-start | bytes 262144 | tf_op jit(solution)/shard_map/all_to_all | solution.py:27
  180.3 2.3 %pad_maximum_fusion = bf16[1024,4,128]{2,0,1:T(8,128)(2,1)} fusion(bf16[512,4,128]{2,0,1:T(8,128)(2,1)} %fusion.17, bf16[512,4,128]{2,0,1:T(8,128)(2,1)} %fusion.16), kind=kLoop, calls=%fused_computation.45 | loop fusion | flops 2097152 | bytes 2097152 | tf_op jit(solution)/shard_map/concatenate | solution.py:118
  182.6 2.3 %copy.67 = bf16[1024,4,128]{0,2,1:T(8,128)(2,1)} copy(bf16[1024,4,128]{2,0,1:T(8,128)(2,1)} %pad_maximum_fusion) | data formatting | bytes 2097152 | tf_op jit(solution)/shard_map/concatenate | solution.py:118
  184.8 2.3 %copy.83 = bf16[1024,512]{1,0:T(8,128)(2,1)} copy(bf16[1024,512]{0,1:T(8,128)(2,1)} %bitcast.142) | data formatting | bytes 2097152
  187.7 4.3 %fusion.11 = bf16[1024,4,128]{0,2,1:T(8,128)(2,1)} fusion(f32[4,1024,128]{1,2,0:T(8,128)S(1)} %fusion.50, f32[4,128,1024]{2,1,0:T(8,128)S(1)} %fusion.29, bf16[512,4,128]{0,2,1:T(8,128)(2,1)} %bitcast.144, bf16[4,512,1024]{2,1,0:T(8,128)(2,1)} %copy-done.1), kind=kOutput, calls=%fused_computation.14 | convolution fusion | flops 538968064 | bytes 9961472 | tf_op jit(solution)/shard_map/cxd,xcr->dcr/dot_general | solution.py:112
  191.9 2.3 %copy.84 = bf16[1024,512]{1,0:T(8,128)(2,1)} copy(bf16[1024,512]{0,1:T(8,128)(2,1)} %bitcast.140) | data formatting | bytes 2097152
  194.2 3.0 %multiply_convert_fusion = bf16[4,128,1024]{2,1,0:T(8,128)(2,1)S(1)} fusion(f32[4,128,1024]{2,1,0:T(8,128)} %fusion.1, f32[4,128,1024]{2,1,0:T(8,128)} %fusion, bf16[4,128,128]{2,1,0:T(8,128)(2,1)S(1)} %reshape_reshape.23, bf16[1024,512]{1,0:T(8,128)(2,1)} %param.6), kind=kOutput, calls=%fused_computation.16 | convolution fusion | flops 136314880 | bytes 6422528 | tf_op jit(solution)/shard_map/jaq,aqd->jad/dot_general | solution.py:88
  (63 shorter events, 28.6 us)
Async XLA Ops:
  7.2 1.2 copy-start
  7.2 16.0 %copy-start.6 = (bf16[1024,512]{1,0:T(8,128)(2,1)S(1)}, bf16[1024,512]{1,0:T(8,128)(2,1)}, u32[]{:S(2)}) copy-start(bf16[1024,512]{1,0:T(8,128)(2,1)} %param.5) | copy-start | bytes 3145732
  7.2 100.3 %all-gather.2.cloned.1.call-start = ((), (), s32[]{:S(2)}) async-start(), calls=%async_computation.8 | async-start | bytes 9437184 | tf_op jit(solution)/shard_map/all_gather | solution.py:44
  18.1 13.2 %all-to-all-start.1 = ((f32[16,2,1,2048]{3,1,2,0:T(2,128)}), f32[16,2,1,2048]{3,1,2,0:T(2,128)S(1)}, u32[]{:S(2)}, u32[]{:S(2)}) async-start(f32[16,2,1,2048]{3,1,2,0:T(2,128)} %copy.57), calls=%async_computation.1 | async-start | bytes 524288 | tf_op jit(solution)/shard_map/all_to_all | solution.py:27
  37.7 10.3 %all-to-all-start.3 = ((bf16[16,2,1,2048]{3,1,2,0:T(2,128)(2,1)}), bf16[16,2,1,2048]{3,1,2,0:T(2,128)(2,1)S(1)}, u32[]{:S(2)}, u32[]{:S(2)}) async-start(bf16[16,2,1,2048]{3,1,2,0:T(2,128)(2,1)} %copy.59), calls=%async_computation.3 | async-start | bytes 262144 | tf_op jit(solution)/shard_map/all_to_all | solution.py:27
  41.5 76.2 %copy-start.10 = (pred[512,1024]{1,0:T(8,128)(4,1)}, pred[512,1024]{1,0:T(8,128)(4,1)S(1)}, u32[]{:S(2)}) copy-start(pred[512,1024]{1,0:T(8,128)(4,1)S(1)} %iota_compare_fusion.1) | copy-start | bytes 1572868
  116.6 1.1 copy-start.8
  117.6 3.9 %copy-start.3 = (bf16[512,512]{0,1:T(8,128)(2,1)}, bf16[512,512]{0,1:T(8,128)(2,1)S(1)}, u32[]{:S(2)}) copy-start(bf16[512,512]{0,1:T(8,128)(2,1)S(1)} %get-tuple-element.14) | copy-start | bytes 1572868
  117.6 1.6 copy-start.4
  119.3 2.2 %copy-start.2 = (bf16[512,512]{0,1:T(8,128)(2,1)S(1)}, bf16[512,512]{0,1:T(8,128)(2,1)}, u32[]{:S(2)}) copy-start(bf16[512,512]{0,1:T(8,128)(2,1)} %copy.75) | copy-start | bytes 1572868
  127.4 4.7 %copy-start.5 = (bf16[1024,512]{1,0:T(8,128)(2,1)S(1)}, bf16[1024,512]{1,0:T(8,128)(2,1)}, u32[]{:S(2)}) copy-start(bf16[1024,512]{1,0:T(8,128)(2,1)} %param.6) | copy-start | bytes 3145732
  130.2 2.0 copy-start.1
  132.1 2.2 %copy-start.7 = (bf16[1024,512]{1,0:T(8,128)(2,1)S(1)}, bf16[1024,512]{1,0:T(8,128)(2,1)}, u32[]{:S(2)}) copy-start(bf16[1024,512]{1,0:T(8,128)(2,1)} %param.5) | copy-start | bytes 3145732
  132.1 2.2 %copy-start.9 = (bf16[1024,512]{0,1:T(8,128)(2,1)S(1)}, bf16[1024,512]{0,1:T(8,128)(2,1)}, u32[]{:S(2)}) copy-start(bf16[1024,512]{0,1:T(8,128)(2,1)} %copy-done.8) | copy-start | bytes 3145732
  144.1 16.7 %all-to-all-start.5 = ((f32[16,2,1,2048]{3,1,2,0:T(2,128)}), f32[16,2,1,2048]{3,1,2,0:T(2,128)S(1)}, u32[]{:S(2)}, u32[]{:S(2)}) async-start(f32[16,2,1,2048]{3,1,2,0:T(2,128)} %copy.71), calls=%async_computation.5 | async-start | bytes 524288 | tf_op jit(solution)/shard_map/all_to_all | solution.py:27
  173.3 13.8 %all-to-all-start.7 = ((bf16[16,2,1,2048]{3,1,2,0:T(2,128)(2,1)}), bf16[16,2,1,2048]{3,1,2,0:T(2,128)(2,1)S(1)}, u32[]{:S(2)}, u32[]{:S(2)}) async-start(bf16[16,2,1,2048]{3,1,2,0:T(2,128)(2,1)} %copy.73), calls=%async_computation.7 | async-start | bytes 262144 | tf_op jit(solution)/shard_map/all_to_all | solution.py:27
Sparse Core Ops, SparseCore 0:
  9.8 97.6 all-gather.1
where the time goes:
time: 207 us; the launch traced here: 205 us
  waiting for transfers between devices  71.4 us (34%)
  matrix products  44.6 us (22%)
  local copies, waits for them, and re-layouts  28.5 us (14%)
  starting transfers between devices  22.2 us (11%)
  blocking collectives  20.3 us (10%)
  between operations  14.3 us (7%)
  other arithmetic  4.08 us (2%)
    all_gather x1, waiting for transfers between devices, local(): lax.all_gather(layer_grad, 'tp', axis=1, tiled=True)  59.4 us
    all_to_all x4, starting transfers between devices, moved_by_axis(): result = lax.all_to_all(result, axes[k], k, k, tiled=True)  22.2 us
    all_to_all x4, blocking collectives, moved_by_axis(): result = lax.all_to_all(result, axes[k], k, k, tiled=True)  20.3 us
    all_to_all x4, waiting for transfers between devices, moved_by_axis(): result = lax.all_to_all(result, axes[k], k, k, tiled=True)  11.3 us
    dot_general x2, matrix products, local(): jnp.einsum('kzx,zkm->xkm', inside_query, gradient_block, preferred_elemen...  10.2 us
    dot_general x1, matrix products, local(): lax.dot_general(lax.all_gather(layer_grad, 'tp', axis=1, tiled=True), out...  9.09 us
    unnamed x25, local copies, waits for them, and re-layouts  8.49 us
    rev x1, local copies, waits for them, and re-layouts, local(): grad_suffix = jnp.cumsum(grad_sources[::-1], 0)[::-1]  5.77 us
  transfers between devices with their start and end apart: 5, of which 3 were waited for; matrix products, arithmetic and copies ran while one was open for 12% of the time, Pallas kernels for 0%

commit v1 on v0

v1 whole, which is shorter than its diff:
```python
import functools

import jax
import jax.numpy as jnp
from jax import lax
from jax.experimental import pallas as pl
from jax.experimental.pallas import tpu as pltpu
from jax.sharding import Mesh
from jax.sharding import PartitionSpec as P


HEAD = 128
CHUNK = 256
CTX = ("y", "x", "core")
F32 = jnp.float32
BF16 = jnp.bfloat16
VMEM_BYTES = 16 * 1024 * 1024
SMALL_BYTES = 4 * 1024 * 1024
VMEM_SPEC = pl.BlockSpec(memory_space=pltpu.VMEM)


def moved(value, axis, by):
    size = lax.axis_size(axis)
    return lax.ppermute(value, axis, [(i, (i + by) % size) for i in range(size)])


def nt(a, b):
    return lax.dot_general(a, b, (((1,), (1,)), ((), ())), preferred_element_type=F32)


def nn(a, b):
    return lax.dot_general(a, b, (((1,), (0,)), ((), ())), preferred_element_type=F32)


def tn(a, b):
    return lax.dot_general(a, b, (((0,), (0,)), ((), ())), preferred_element_type=F32)


def upper():
    rows = lax.broadcasted_iota(jnp.int32, (CHUNK, CHUNK), 0)
    cols = lax.broadcasted_iota(jnp.int32, (CHUNK, CHUNK), 1)
    return rows <= cols


def call(kernel, ins, outs, flops=0, scratch=(), limit=VMEM_BYTES, in_specs=None, out_specs=None):
    shapes = [jax.ShapeDtypeStruct(*out) for out in outs]
    moved_bytes = sum(a.size * a.dtype.itemsize for a in (*ins, *shapes))
    return pl.pallas_call(
        kernel,
        in_specs=in_specs or [VMEM_SPEC] * len(ins),
        out_specs=out_specs or [VMEM_SPEC] * len(outs),
        out_shape=shapes,
        scratch_shapes=scratch,
        compiler_params=pltpu.CompilerParams(vmem_limit_bytes=limit),
        cost_estimate=pl.CostEstimate(flops=flops, bytes_accessed=moved_bytes, transcendentals=0),
    )(*ins)


def before_kernel(heads, q_ref, k_ref, v_ref, inner_ref, parts_ref, mine_ref, theirs_ref, total_ref):
    keep = upper()
    for h in range(heads):
        cols = slice(h * HEAD, (h + 1) * HEAD)
        total = None
        for i in range(q_ref.shape[0] // CHUNK):
            rows = pl.ds(i * CHUNK, CHUNK)
            k = k_ref[rows, cols]
            inner_ref[h, i] = jnp.where(keep, nt(k, q_ref[rows, cols]), 0.0).astype(BF16)
            part = tn(k, v_ref[rows, cols])
            parts_ref[h, i] = part
            total = part if total is None else total + part
        total_ref[h] = total
    share(total_ref, mine_ref, theirs_ref)


def before(q, k, v, heads, wire):
    tokens = q.shape[0]
    chunks = tokens // CHUNK
    half = (heads // 2, HEAD, HEAD)
    return call(
        functools.partial(before_kernel, heads),
        (q, k, v),
        (
            ((heads, chunks, CHUNK, CHUNK), BF16),
            ((heads, chunks, HEAD, HEAD), F32),
            (half, F32),
            (half, wire),
        ),
        flops=heads * tokens * (CHUNK + HEAD) * HEAD * 2,
        scratch=[pltpu.VMEM((heads, HEAD, HEAD), F32)],
    )


PIECES = 4


def split_kernel(x_ref, lo_ref, hi_ref, sems):
    step = lo_ref.shape[0] // PIECES
    copies = []
    for half, ref in enumerate((lo_ref, hi_ref)):
        for i in range(PIECES):
            src = x_ref.at[pl.ds(half * lo_ref.shape[0] + i * step, step), :]
            copies.append(
                pltpu.make_async_copy(src, ref.at[pl.ds(i * step, step), :], sems.at[len(copies)])
            )
            copies[-1].start()
    for copy in copies:
        copy.wait()


def split(x):
    half = ((x.shape[0] // 2, x.shape[1]), x.dtype)
    return call(
        split_kernel,
        (pltpu.with_memory_space_constraint(x, pltpu.HBM),),
        (half, half),
        scratch=[pltpu.SemaphoreType.DMA((2 * PIECES,))],
        limit=SMALL_BYTES,
        in_specs=[pl.BlockSpec(memory_space=pltpu.HBM)],
    )


def weight_of(w_ref, by):
    size = lax.axis_size("tp")
    width = w_ref.shape[1] // size
    source = lax.rem(lax.axis_index("tp") + by + size, size)
    return w_ref[:, pl.ds(pl.multiple_of(source * width, width), width)]


def product_kernel(offsets, w_ref, *refs):
    out_ref = refs[-1]
    total = refs[len(offsets)][...] if len(refs) > len(offsets) + 1 else None
    for by, ref in zip(offsets, refs):
        term = nt(ref[...], weight_of(w_ref, by))
        total = term if total is None else total + term
    out_ref[...] = total


def product(w, parts, offsets, total):
    rows, width = parts[0].shape
    ins = (w, *parts) if total is None else (w, *parts, total)
    (out,) = call(
        functools.partial(product_kernel, offsets),
        ins,
        (((rows, w.shape[0]), F32),),
        flops=2 * rows * width * w.shape[0] * len(parts),
    )
    return out


def share(total_ref, mine_ref, theirs_ref):
    core = lax.axis_index("core")
    half = mine_ref.shape[0]
    for i in range(half):
        mine_ref[i] = total_ref[core * half + i]
        theirs_ref[i] = total_ref[(1 - core) * half + i].astype(theirs_ref.dtype)


def grads_kernel(heads, acc_lo, acc_hi, x_lo, x_hi, w_ref, q_ref, g_ref, parts_ref, mine_ref, theirs_ref, total_ref):
    tokens = q_ref.shape[0]
    chunks = tokens // CHUNK
    far = weight_of(w_ref, lax.axis_size("tp") // 2)
    totals = [None] * heads
    for i in range(chunks):
        acc_ref, x_ref = (acc_lo, x_lo) if i < chunks // 2 else (acc_hi, x_hi)
        near = pl.ds(i % (chunks // 2) * CHUNK, CHUNK)
        rows = pl.ds(i * CHUNK, CHUNK)
        g = (acc_ref[near, :] + nt(x_ref[near, :], far)).astype(BF16)
        g_ref[rows, :] = g
        for h in range(heads):
            cols = slice(h * HEAD, (h + 1) * HEAD)
            part = tn(q_ref[rows, cols], g[:, cols])
            parts_ref[h, i] = part
            totals[h] = part if i == 0 else totals[h] + part
    for h in range(heads):
        total_ref[h] = totals[h]
    share(total_ref, mine_ref, theirs_ref)


def grads(totals, last, w, q, heads, wire):
    tokens, columns = q.shape
    half = (heads // 2, HEAD, HEAD)
    return call(
        functools.partial(grads_kernel, heads),
        (*totals, *last, w, q),
        (
            ((tokens, columns), BF16),
            ((heads, tokens // CHUNK, HEAD, HEAD), F32),
            (half, F32),
            (half, wire),
        ),
        flops=2 * tokens * columns * (columns + HEAD),
        scratch=[pltpu.VMEM((heads, HEAD, HEAD), F32)],
    )


def pair_kernel(mine_ref, partner_ref, sent_ref):
    sent_ref[...] = (mine_ref[...] + partner_ref[...].astype(F32)).astype(sent_ref.dtype)


def counted(axis, later, refs):
    here, size = lax.axis_index(axis), lax.axis_size(axis)
    outer = total = None
    for by, ref in enumerate(refs, 1):
        got = ref[...].astype(F32)
        source = lax.rem(here - by + size, size)
        keep = source > here if later else source < here
        term = jnp.where(keep, got, 0.0)
        outer = term if outer is None else outer + term
        total = got if total is None else total + got
    return outer, total


def row_kernel(axis, later, mine_ref, partner_ref, *refs):
    outer_ref, sent_ref = refs[-2:]
    outer, total = counted(axis, later, refs[:-2])
    outer_ref[...] = outer
    sent_ref[...] = (total + mine_ref[...] + partner_ref[...].astype(F32)).astype(sent_ref.dtype)


def last_kernel(axis, later, mine_ref, partner_ref, outer_ref, *refs):
    me_ref, them_ref = refs[-2:]
    outer, _ = counted(axis, later, refs[:-2])
    outer = outer + outer_ref[...]
    inner = lax.axis_index("core") == (0 if later else 1)
    me_ref[...] = (outer + jnp.where(inner, partner_ref[...].astype(F32), 0.0)).astype(BF16)
    them_ref[...] = (outer + jnp.where(inner, 0.0, mine_ref[...])).astype(BF16)


def summed(mine, theirs, later):
    shape, wire = mine.shape, theirs.dtype
    partner = moved(theirs, "core", 1)
    (sent,) = call(pair_kernel, (mine, partner), ((shape, wire),), limit=SMALL_BYTES)
    got = [moved(sent, "x", by) for by in range(1, lax.axis_size("x"))]
    outer, sent = call(
        functools.partial(row_kernel, "x", later),
        (mine, partner, *got),
        ((shape, F32), (shape, wire)),
        limit=SMALL_BYTES,
    )
    got = [moved(sent, "y", by) for by in range(1, lax.axis_size("y"))]
    for_me, for_them = call(
        functools.partial(last_kernel, "y", later),
        (mine, partner, outer, *got),
        ((shape, BF16), (shape, BF16)),
        limit=SMALL_BYTES,
    )
    return for_me, moved(for_them, "core", 1)


def state_of(h, mine_ref, other_ref):
    half = mine_ref.shape[0]
    mine = lax.axis_index("core") == h // half
    return jnp.where(mine, mine_ref[h % half].astype(F32), other_ref[h % half].astype(F32))


def inside_kernel(factor, h, q_ref, k_ref, v_ref, g_ref, inner_ref, parts_ref, mine_ref, other_ref, qg_ref, kg_ref, vg_ref):
    keep = upper()
    state = state_of(h, mine_ref, other_ref)
    cols = slice(h * HEAD, (h + 1) * HEAD)
    for i in range(q_ref.shape[0] // CHUNK):
        rows = pl.ds(i * CHUNK, CHUNK)
        q, k, v, g = q_ref[rows, cols], k_ref[rows, cols], v_ref[rows, cols], g_ref[rows, cols]
        down = jnp.where(keep, nt(v, g), 0.0).astype(BF16)
        qg = tn(down, k) + nt(g, state.astype(BF16))
        qg_ref[rows, :] = (factor * qg).astype(BF16)
        kg_ref[rows, :] = nn(down, q)
        vg_ref[rows, :] = nn(inner_ref[h, i], g)
        state = state + parts_ref[h, i]


def inside(h, factor, q, k, v, g, inner, parts, states):
    shape = (q.shape[0], HEAD)
    return call(
        functools.partial(inside_kernel, factor, h),
        (q, k, v, g, inner, parts, *states),
        ((shape, BF16), (shape, F32), (shape, F32)),
        flops=q.shape[0] * HEAD * (4 * CHUNK + HEAD) * 2,
    )


def outside_kernel(factor, heads, *refs):
    qg_refs, kg_refs, vg_refs = (refs[i * heads : (i + 1) * heads] for i in range(3))
    k_ref, v_ref, parts_ref, mine_ref, other_ref, query_out, key_out, value_out, key_buf, value_buf, sems = refs[3 * heads :]
    copies = []

    def send(src, dst):
        copies.append(pltpu.make_async_copy(src, dst, sems.at[len(copies)]))
        copies[-1].start()

    for h in range(heads):
        send(qg_refs[h], query_out.at[:, pl.ds(h * HEAD, HEAD)])
    chunks = k_ref.shape[0] // CHUNK
    after = [state_of(h, mine_ref, other_ref) for h in range(heads)]
    for i in reversed(range(chunks)):
        rows = pl.ds(i * CHUNK, CHUNK)
        for h in range(heads):
            cols = slice(h * HEAD, (h + 1) * HEAD)
            state = after[h].astype(BF16)
            key = kg_refs[h][rows, :] + nt(v_ref[rows, cols], state)
            value = vg_refs[h][rows, :] + nn(k_ref[rows, cols], state)
            key_buf[rows, cols] = (factor * key).astype(BF16)
            value_buf[rows, cols] = (factor * value).astype(BF16)
            if i:
                after[h] = after[h] + parts_ref[h, i]
        send(key_buf.at[rows, :], key_out.at[rows, :])
        send(value_buf.at[rows, :], value_out.at[rows, :])
    for copy in copies:
        copy.wait()


def outside(factor, qg, kg, vg, k, v, parts, states):
    heads = len(qg)
    tokens, columns = k.shape
    return call(
        functools.partial(outside_kernel, factor, heads),
        (*qg, *kg, *vg, k, v, parts, *states),
        ((k.shape, BF16),) * 3,
        flops=4 * tokens * columns * HEAD,
        scratch=[
            pltpu.VMEM(k.shape, BF16),
            pltpu.VMEM(k.shape, BF16),
            pltpu.SemaphoreType.DMA((heads + 2 * (tokens // CHUNK),)),
        ],
        out_specs=[pl.BlockSpec(memory_space=pl.ANY)] * 3,
    )


def body(query_rows, key_rows, value_rows, layer_grad, out_weight):
    tokens, columns = query_rows.shape
    heads = columns // HEAD
    factor = float((HEAD * tokens * lax.axis_size(CTX)) ** (-0.5))
    hops = lax.axis_size("tp") // 2

    right = list(split(layer_grad))
    left = list(right)
    parts, offsets, totals = [[part] for part in right], [0], [None, None]
    for hop in range(1, hops):
        right = [moved(right[i], "tp", 1) for i in (0, 1)]
        left = [moved(left[i], "tp", -1) for i in (1, 0)][::-1]
        offsets = offsets + [-hop, hop]
        totals = [product(out_weight, parts[i] + [right[i], left[i]], offsets, totals[i]) for i in (0, 1)]
        parts, offsets = [[], []], []
    last = [moved(right[0], "tp", 1), moved(left[1], "tp", -1)]

    inner, kv_parts, kv_mine, kv_theirs = before(query_rows, key_rows, value_rows, heads, F32)
    kv_states = summed(kv_mine, kv_theirs, False)

    g, g_parts, g_mine, g_theirs = grads(totals, last, out_weight, query_rows, heads, BF16)
    states = summed(g_mine, g_theirs, True)

    near = []
    for h in range(heads):
        near.append(
            inside(h, factor, query_rows, key_rows, value_rows, g, inner, kv_parts, kv_states)
        )
    qg, kg, vg = zip(*near)
    return outside(factor, qg, kg, vg, key_rows, value_rows, g_parts, states)


def solution(mesh):
    finer = Mesh(mesh.devices.reshape(4, 4, 2, mesh.shape["tp"]), (*CTX, "tp"))
    return jax.shard_map(
        body,
        mesh=finer,
        in_specs=(P(CTX, "tp"), P(CTX, "tp"), P(CTX, "tp"), P(CTX, "tp"), P("tp", None)),
        out_specs=(P(CTX, "tp"), P(CTX, "tp"), P(CTX, "tp")),
        check_vma=False,
    )
```

time: 207 us -> 117 us (0.57)
  matrix products: 44.6 us -> 0 us
  local copies, waits for them, and re-layouts: 28.5 us -> 3.69 us
  starting transfers between devices: 22.2 us -> 46.4 us
  waiting for transfers between devices: 71.4 us -> 49.9 us
  blocking collectives: 20.3 us -> 0 us
  Pallas kernels: 0 us -> 15.9 us
  between operations: 14.3 us -> 1 us
  other arithmetic: 4.08 us -> 0 us
    all_gather x1 -> x0, waiting for transfers between devices: 59.4 us -> none  [local(): lax.all_gather(layer_grad, 'tp', axis=1, tiled=True)]
    ppermute x0 -> x30, waiting for transfers between devices: none -> 49.9 us  [moved(): lax.ppermute(value, axis, [(i, (i + by) % size) for i in range(size)])]
    ppermute x0 -> x30, starting transfers between devices: none -> 46.4 us  [moved(): lax.ppermute(value, axis, [(i, (i + by) % size) for i in range(size)])]
    dot_general x15 -> x0, matrix products: 44.6 us -> none  [the longest x2 10.2 us: local(): jnp.einsum('kzx,zkm->xkm', inside_query, gradient_block, preferred_elemen...]
    all_to_all x4 -> x0, starting transfers between devices: 22.2 us -> none  [moved_by_axis(): result = lax.all_to_all(result, axes[k], k, k, tiled=True)]
    all_to_all x4 -> x0, blocking collectives: 20.3 us -> none  [moved_by_axis(): result = lax.all_to_all(result, axes[k], k, k, tiled=True)]
    pallas_call x0 -> x20, Pallas kernels: none -> 15.9 us  [call(): pl.pallas_call(kernel, in_specs=in_specs or [VMEM_SPEC] * len(ins), out_s...]
    all_to_all x4 -> x0, waiting for transfers between devices: 11.3 us -> none  [moved_by_axis(): result = lax.all_to_all(result, axes[k], k, k, tiled=True)]
  transfers between devices with their start and end apart: 5 -> 30, of which waited for: 3 -> 13; matrix products, arithmetic and copies ran while one was open for 12% -> 0% of each run, Pallas kernels for 0% -> 11%
where the time goes in v1:
time: 117 us
  waiting for transfers between devices  49.9 us (43%)
  starting transfers between devices  46.4 us (40%)
  Pallas kernels  15.9 us (14%)
  local copies, waits for them, and re-layouts  3.69 us (3%)
    ppermute x30, waiting for transfers between devices, moved(): lax.ppermute(value, axis, [(i, (i + by) % size) for i in range(size)])  49.9 us
    ppermute x30, starting transfers between devices, moved(): lax.ppermute(value, axis, [(i, (i + by) % size) for i in range(size)])  46.4 us
    pallas_call x20, Pallas kernels, call(): pl.pallas_call(kernel, in_specs=in_specs or [VMEM_SPEC] * len(ins), out_s...  15.9 us
    unnamed x12, local copies, waits for them, and re-layouts  3.69 us
  transfers between devices with their start and end apart: 30, of which 13 were waited for; matrix products, arithmetic and copies ran while one was open for 0% of the time, Pallas kernels for 11%

profile of v1, /device:TPU:1, one launch (start us, length us, event | category | flops | bytes accessed | tf_op | source)
XLA Modules:
  0.0 116.8 jit_solution(18433612685205899362)
XLA Ops:
  2.1 2.5 %collective-permute-start = (bf16[512,512]{1,0:T(8,128)(2,1)S(1)}, bf16[512,512]{1,0:T(8,128)(2,1)S(1)}, u32[]{:S(2)}, u32[]{:S(2)}) collective-permute-start(bf16[512,512]{1,0:T(8,128)(2,1)S(1)} %get-tuple-element.33.refs_0_), channel_id=1, source_target_pairs={{0,1},{1,2},{2,3},{3,4},{4,5},{5,6},{6,7},{7,0},{8,9},{9,10},{10,1... | collective-permute-start | bytes 1572872 | tf_op jit(solution)/shard_map/ppermute | solution.py:24
  4.7 4.0 %collective-permute-start.9 = (bf16[512,512]{1,0:T(8,128)(2,1)S(1)}, bf16[512,512]{1,0:T(8,128)(2,1)S(1)}, u32[]{:S(2)}, u32[]{:S(2)}) collective-permute-start(bf16[512,512]{1,0:T(8,128)(2,1)S(1)} %get-tuple-element.34.refs_0_), channel_id=1, source_target_pairs={{0,7},{1,0},{2,1},{3,2},{4,3},{5,4},{6,5},{7,6},{8,15},{9,8},{10,9... | collective-permute-start | bytes 1572872 | tf_op jit(solution)/shard_map/ppermute | solution.py:24
  10.2 10.1 %collective-permute-done.refs_1_ = bf16[512,512]{1,0:T(8,128)(2,1)S(1)} collective-permute-done((bf16[512,512]{1,0:T(8,128)(2,1)S(1)}, bf16[512,512]{1,0:T(8,128)(2,1)S(1)}, u32[]{:S(2)}, u32[]{:S(2)}) %collective-permute-start) | collective-permute-done | bytes 524320 | tf_op jit(solution)/shard_map/ppermute | solution.py:24
  20.2 2.7 %collective-permute-start.10 = (bf16[512,512]{1,0:T(8,128)(2,1)S(1)}, bf16[512,512]{1,0:T(8,128)(2,1)S(1)}, u32[]{:S(2)}, u32[]{:S(2)}) collective-permute-start(bf16[512,512]{1,0:T(8,128)(2,1)S(1)} %collective-permute-done.9.refs_2_), channel_id=1, source_target_pairs={{0,7},{1,0},{2,1},{3,2},{4,3},{5,4},{6,5},{7,6},{8,15},{9,8},{10,9... | collective-permute-start | bytes 1572872 | tf_op jit(solution)/shard_map/ppermute | solution.py:24
  22.9 7.6 %collective-permute-done.3.refs_2_ = bf16[512,512]{1,0:T(8,128)(2,1)S(1)} collective-permute-done((bf16[512,512]{1,0:T(8,128)(2,1)S(1)}, bf16[512,512]{1,0:T(8,128)(2,1)S(1)}, u32[]{:S(2)}, u32[]{:S(2)}) %collective-permute-start.3) | collective-permute-done | bytes 524320 | tf_op jit(solution)/shard_map/ppermute | solution.py:24
  30.5 3.4 %collective-permute-start.4 = (bf16[512,512]{1,0:T(8,128)(2,1)S(1)}, bf16[512,512]{1,0:T(8,128)(2,1)S(1)}, u32[]{:S(2)}, u32[]{:S(2)}) collective-permute-start(bf16[512,512]{1,0:T(8,128)(2,1)S(1)} %collective-permute-done.3.refs_2_), channel_id=1, source_target_pairs={{0,7},{1,0},{2,1},{3,2},{4,3},{5,4},{6,5},{7,6},{8,15},{9,8},{10,9... | collective-permute-start | bytes 1572872 | tf_op jit(solution)/shard_map/ppermute | solution.py:24
  34.0 8.7 %collective-permute-done.1.refs_0_ = bf16[512,512]{1,0:T(8,128)(2,1)S(1)} collective-permute-done((bf16[512,512]{1,0:T(8,128)(2,1)S(1)}, bf16[512,512]{1,0:T(8,128)(2,1)S(1)}, u32[]{:S(2)}, u32[]{:S(2)}) %collective-permute-start.1) | collective-permute-done | bytes 524320 | tf_op jit(solution)/shard_map/ppermute | solution.py:24
  42.7 2.7 %collective-permute-start.11 = (bf16[512,512]{1,0:T(8,128)(2,1)S(1)}, bf16[512,512]{1,0:T(8,128)(2,1)S(1)}, u32[]{:S(2)}, u32[]{:S(2)}) collective-permute-start(bf16[512,512]{1,0:T(8,128)(2,1)S(1)} %collective-permute-done.10.refs_1_), channel_id=1, source_target_pairs={{0,7},{1,0},{2,1},{3,2},{4,3},{5,4},{6,5},{7,6},{8,15},{9,8},{10,9... | collective-permute-start | bytes 1572872 | tf_op jit(solution)/shard_map/ppermute | solution.py:24
  50.1 2.8 %collective-permute-start.14 = (f32[2,128,128]{2,1,0:T(8,128)S(1)}, f32[2,128,128]{2,1,0:T(8,128)S(1)}, u32[]{:S(2)}, u32[]{:S(2)}) collective-permute-start(f32[2,128,128]{2,1,0:T(8,128)S(1)} %get-tuple-element.39), channel_id=1, source_target_pairs={{0,8},{8,0},{1,9},{9,1},{2,10},{10,2},{3,11},{11,3},{4,12},{12,4},... | collective-permute-start | bytes 393224 | tf_op jit(solution)/shard_map/ppermute | solution.py:24
  54.0 2.6 %collective-permute-start.17 = (f32[2,128,128]{2,1,0:T(8,128)S(1)}, f32[2,128,128]{2,1,0:T(8,128)S(1)}, u32[]{:S(2)}, u32[]{:S(2)}) collective-permute-start(f32[2,128,128]{2,1,0:T(8,128)S(1)} %shard_map.85), channel_id=1, source_target_pairs={{0,48},{16,0},{32,16},{48,32},{1,49},{17,1},{33,17},{49,33},{2,50}... | collective-permute-start | bytes 393224 | tf_op jit(solution)/shard_map/ppermute | solution.py:24
  57.0 2.0 %collective-permute-done.17.refs_2_ = f32[2,128,128]{2,1,0:T(8,128)S(1)} collective-permute-done((f32[2,128,128]{2,1,0:T(8,128)S(1)}, f32[2,128,128]{2,1,0:T(8,128)S(1)}, u32[]{:S(2)}, u32[]{:S(2)}) %collective-permute-start.17) | collective-permute-done | bytes 131104 | tf_op jit(solution)/shard_map/ppermute | solution.py:24
  59.0 2.5 %collective-permute-start.16 = (f32[2,128,128]{2,1,0:T(8,128)S(1)}, f32[2,128,128]{2,1,0:T(8,128)S(1)}, u32[]{:S(2)}, u32[]{:S(2)}) collective-permute-start(f32[2,128,128]{2,1,0:T(8,128)S(1)} %shard_map.85), channel_id=1, source_target_pairs={{0,32},{16,48},{32,0},{48,16},{1,33},{17,49},{33,1},{49,17},{2,34}... | collective-permute-start | bytes 393224 | tf_op jit(solution)/shard_map/ppermute | solution.py:24
  61.5 3.7 %collective-permute-done.2.refs_0_ = bf16[512,512]{1,0:T(8,128)(2,1)S(1)} collective-permute-done((bf16[512,512]{1,0:T(8,128)(2,1)S(1)}, bf16[512,512]{1,0:T(8,128)(2,1)S(1)}, u32[]{:S(2)}, u32[]{:S(2)}) %collective-permute-start.2) | collective-permute-done | bytes 524320 | tf_op jit(solution)/shard_map/ppermute | solution.py:24
  65.2 2.7 %collective-permute-start.13 = (bf16[512,512]{1,0:T(8,128)(2,1)S(1)}, bf16[512,512]{1,0:T(8,128)(2,1)S(1)}, u32[]{:S(2)}, u32[]{:S(2)}) collective-permute-start(bf16[512,512]{1,0:T(8,128)(2,1)S(1)} %collective-permute-done.11.refs_1_), channel_id=1, source_target_pairs={{0,7},{1,0},{2,1},{3,2},{4,3},{5,4},{6,5},{7,6},{8,15},{9,8},{10,9... | collective-permute-start | bytes 1572872 | tf_op jit(solution)/shard_map/ppermute | solution.py:24
  69.1 4.1 %collective-permute-done.15.refs_0_ = f32[2,128,128]{2,1,0:T(8,128)S(1)} collective-permute-done((f32[2,128,128]{2,1,0:T(8,128)S(1)}, f32[2,128,128]{2,1,0:T(8,128)S(1)}, u32[]{:S(2)}, u32[]{:S(2)}) %collective-permute-start.15) | collective-permute-done | bytes 131104 | tf_op jit(solution)/shard_map/ppermute | solution.py:24
  73.3 2.8 %collective-permute-start.20 = (f32[2,128,128]{2,1,0:T(8,128)S(1)}, f32[2,128,128]{2,1,0:T(8,128)S(1)}, u32[]{:S(2)}, u32[]{:S(2)}) collective-permute-start(f32[2,128,128]{2,1,0:T(8,128)S(1)} %get-tuple-element.41), channel_id=1, source_target_pairs={{0,192},{64,0},{128,64},{192,128},{1,193},{65,1},{129,65},{193,129... | collective-permute-start | bytes 393224 | tf_op jit(solution)/shard_map/ppermute | solution.py:24
  82.4 4.8 %collective-permute-done.12.x_lo = bf16[512,512]{1,0:T(8,128)(2,1)S(1)} collective-permute-done((bf16[512,512]{1,0:T(8,128)(2,1)S(1)}, bf16[512,512]{1,0:T(8,128)(2,1)S(1)}, u32[]{:S(2)}, u32[]{:S(2)}) %collective-permute-start.12) | collective-permute-done | bytes 524320 | tf_op jit(solution)/shard_map/ppermute | solution.py:24
  87.2 1.8 %shard_map.83 = (bf16[1024,512]{1,0:T(8,128)(2,1)S(1)}, f32[4,4,128,128]{3,2,1,0:T(8,128)S(1)}, f32[2,128,128]{2,1,0:T(8,128)S(1)}, bf16[2,128,128]{2,1,0:T(8,128)(2,1)S(1)}) custom-call(f32[512,512]{1,0:T(8,128)S(1)} %shard_map.79.acc_lo, f32[512,512]{1,0:T(8,128)S(1)} %shard_map.82.acc_hi, bf16[512,512]{1,0:T(8,128)(2,1)S(1)} %collective-permute-done.12.x_lo, ...), custom_call_target="tpu_custom_call" | custom-call | flops 671088640 | bytes 10682368 | tf_op jit(solution)/shard_map/pallas_call | solution.py:48
  89.0 1.8 %collective-permute-start.22 = (bf16[2,128,128]{2,1,0:T(8,128)(2,1)S(1)}, bf16[2,128,128]{2,1,0:T(8,128)(2,1)S(1)}, u32[]{:S(2)}, u32[]{:S(2)}) collective-permute-start(bf16[2,128,128]{2,1,0:T(8,128)(2,1)S(1)} %get-tuple-element.58), channel_id=1, source_target_pairs={{0,8},{8,0},{1,9},{9,1},{2,10},{10,2},{3,11},{11,3},{4,12},{12,4},... | collective-permute-start | bytes 196616 | tf_op jit(solution)/shard_map/ppermute | solution.py:24
  91.7 2.6 %collective-permute-start.25 = (bf16[2,128,128]{2,1,0:T(8,128)(2,1)S(1)}, bf16[2,128,128]{2,1,0:T(8,128)(2,1)S(1)}, u32[]{:S(2)}, u32[]{:S(2)}) collective-permute-start(bf16[2,128,128]{2,1,0:T(8,128)(2,1)S(1)} %shard_map.92), channel_id=1, source_target_pairs={{0,48},{16,0},{32,16},{48,32},{1,49},{17,1},{33,17},{49,33},{2,50}... | collective-permute-start | bytes 196616 | tf_op jit(solution)/shard_map/ppermute | solution.py:24
  96.9 2.0 %collective-permute-done.24.refs_1_ = bf16[2,128,128]{2,1,0:T(8,128)(2,1)S(1)} collective-permute-done((bf16[2,128,128]{2,1,0:T(8,128)(2,1)S(1)}, bf16[2,128,128]{2,1,0:T(8,128)(2,1)S(1)}, u32[]{:S(2)}, u32[]{:S(2)}) %collective-permute-start.24) | collective-permute-done | bytes 65568 | tf_op jit(solution)/shard_map/ppermute | solution.py:24
  100.7 2.8 %collective-permute-start.28 = (bf16[2,128,128]{2,1,0:T(8,128)(2,1)S(1)}, bf16[2,128,128]{2,1,0:T(8,128)(2,1)S(1)}, u32[]{:S(2)}, u32[]{:S(2)}) collective-permute-start(bf16[2,128,128]{2,1,0:T(8,128)(2,1)S(1)} %get-tuple-element.60), channel_id=1, source_target_pairs={{0,192},{64,0},{128,64},{192,128},{1,193},{65,1},{129,65},{193,129... | collective-permute-start | bytes 196616 | tf_op jit(solution)/shard_map/ppermute | solution.py:24
  105.7 2.5 %collective-permute-done.27.refs_1_ = bf16[2,128,128]{2,1,0:T(8,128)(2,1)S(1)} collective-permute-done((bf16[2,128,128]{2,1,0:T(8,128)(2,1)S(1)}, bf16[2,128,128]{2,1,0:T(8,128)(2,1)S(1)}, u32[]{:S(2)}, u32[]{:S(2)}) %collective-permute-start.27) | collective-permute-done | bytes 65568 | tf_op jit(solution)/shard_map/ppermute | solution.py:24
  108.9 2.6 %collective-permute-start.29 = (bf16[2,128,128]{2,1,0:T(8,128)(2,1)S(1)}, bf16[2,128,128]{2,1,0:T(8,128)(2,1)S(1)}, u32[]{:S(2)}, u32[]{:S(2)}) collective-permute-start(bf16[2,128,128]{2,1,0:T(8,128)(2,1)S(1)} %get-tuple-element.62), channel_id=1, source_target_pairs={{0,8},{8,0},{1,9},{9,1},{2,10},{10,2},{3,11},{11,3},{4,12},{12,4},... | collective-permute-start | bytes 196616 | tf_op jit(solution)/shard_map/ppermute | solution.py:24
  (68 shorter events, 30.1 us)
Async XLA Ops:
  2.1 18.1 %collective-permute-start = (bf16[512,512]{1,0:T(8,128)(2,1)S(1)}, bf16[512,512]{1,0:T(8,128)(2,1)S(1)}, u32[]{:S(2)}, u32[]{:S(2)}) collective-permute-start(bf16[512,512]{1,0:T(8,128)(2,1)S(1)} %get-tuple-element.33.refs_0_), channel_id=1, source_target_pairs={{0,1},{1,2},{2,3},{3,4},{4,5},{5,6},{6,7},{7,0},{8,9},{9,10},{10,1... | collective-permute-start | bytes 1572872 | tf_op jit(solution)/shard_map/ppermute | solution.py:24
  4.7 15.6 %collective-permute-start.9 = (bf16[512,512]{1,0:T(8,128)(2,1)S(1)}, bf16[512,512]{1,0:T(8,128)(2,1)S(1)}, u32[]{:S(2)}, u32[]{:S(2)}) collective-permute-start(bf16[512,512]{1,0:T(8,128)(2,1)S(1)} %get-tuple-element.34.refs_0_), channel_id=1, source_target_pairs={{0,7},{1,0},{2,1},{3,2},{4,3},{5,4},{6,5},{7,6},{8,15},{9,8},{10,9... | collective-permute-start | bytes 1572872 | tf_op jit(solution)/shard_map/ppermute | solution.py:24
  8.7 21.8 %collective-permute-start.3 = (bf16[512,512]{1,0:T(8,128)(2,1)S(1)}, bf16[512,512]{1,0:T(8,128)(2,1)S(1)}, u32[]{:S(2)}, u32[]{:S(2)}) collective-permute-start(bf16[512,512]{1,0:T(8,128)(2,1)S(1)} %get-tuple-element.33.refs_0_), channel_id=1, source_target_pairs={{0,7},{1,0},{2,1},{3,2},{4,3},{5,4},{6,5},{7,6},{8,15},{9,8},{10,9... | collective-permute-start | bytes 1572872 | tf_op jit(solution)/shard_map/ppermute | solution.py:24
  10.1 23.9 %collective-permute-start.6 = (bf16[512,512]{1,0:T(8,128)(2,1)S(1)}, bf16[512,512]{1,0:T(8,128)(2,1)S(1)}, u32[]{:S(2)}, u32[]{:S(2)}) collective-permute-start(bf16[512,512]{1,0:T(8,128)(2,1)S(1)} %get-tuple-element.34.refs_0_), channel_id=1, source_target_pairs={{0,1},{1,2},{2,3},{3,4},{4,5},{5,6},{6,7},{7,0},{8,9},{9,10},{10,1... | collective-permute-start | bytes 1572872 | tf_op jit(solution)/shard_map/ppermute | solution.py:24
  20.2 22.5 %collective-permute-start.1 = (bf16[512,512]{1,0:T(8,128)(2,1)S(1)}, bf16[512,512]{1,0:T(8,128)(2,1)S(1)}, u32[]{:S(2)}, u32[]{:S(2)}) collective-permute-start(bf16[512,512]{1,0:T(8,128)(2,1)S(1)} %collective-permute-done.refs_1_), channel_id=1, source_target_pairs={{0,1},{1,2},{2,3},{3,4},{4,5},{5,6},{6,7},{7,0},{8,9},{9,10},{10,1... | collective-permute-start | bytes 1572872 | tf_op jit(solution)/shard_map/ppermute | solution.py:24
  20.2 22.5 %collective-permute-start.10 = (bf16[512,512]{1,0:T(8,128)(2,1)S(1)}, bf16[512,512]{1,0:T(8,128)(2,1)S(1)}, u32[]{:S(2)}, u32[]{:S(2)}) collective-permute-start(bf16[512,512]{1,0:T(8,128)(2,1)S(1)} %collective-permute-done.9.refs_2_), channel_id=1, source_target_pairs={{0,7},{1,0},{2,1},{3,2},{4,3},{5,4},{6,5},{7,6},{8,15},{9,8},{10,9... | collective-permute-start | bytes 1572872 | tf_op jit(solution)/shard_map/ppermute | solution.py:24
  30.5 26.0 %collective-permute-start.4 = (bf16[512,512]{1,0:T(8,128)(2,1)S(1)}, bf16[512,512]{1,0:T(8,128)(2,1)S(1)}, u32[]{:S(2)}, u32[]{:S(2)}) collective-permute-start(bf16[512,512]{1,0:T(8,128)(2,1)S(1)} %collective-permute-done.3.refs_2_), channel_id=1, source_target_pairs={{0,7},{1,0},{2,1},{3,2},{4,3},{5,4},{6,5},{7,6},{8,15},{9,8},{10,9... | collective-permute-start | bytes 1572872 | tf_op jit(solution)/shard_map/ppermute | solution.py:24
  34.0 27.5 %collective-permute-start.7 = (bf16[512,512]{1,0:T(8,128)(2,1)S(1)}, bf16[512,512]{1,0:T(8,128)(2,1)S(1)}, u32[]{:S(2)}, u32[]{:S(2)}) collective-permute-start(bf16[512,512]{1,0:T(8,128)(2,1)S(1)} %collective-permute-done.6.refs_1_), channel_id=1, source_target_pairs={{0,1},{1,2},{2,3},{3,4},{4,5},{5,6},{6,7},{7,0},{8,9},{9,10},{10,1... | collective-permute-start | bytes 1572872 | tf_op jit(solution)/shard_map/ppermute | solution.py:24
  42.7 22.5 %collective-permute-start.2 = (bf16[512,512]{1,0:T(8,128)(2,1)S(1)}, bf16[512,512]{1,0:T(8,128)(2,1)S(1)}, u32[]{:S(2)}, u32[]{:S(2)}) collective-permute-start(bf16[512,512]{1,0:T(8,128)(2,1)S(1)} %collective-permute-done.1.refs_0_), channel_id=1, source_target_pairs={{0,1},{1,2},{2,3},{3,4},{4,5},{5,6},{6,7},{7,0},{8,9},{9,10},{10,1... | collective-permute-start | bytes 1572872 | tf_op jit(solution)/shard_map/ppermute | solution.py:24
  42.7 22.5 %collective-permute-start.11 = (bf16[512,512]{1,0:T(8,128)(2,1)S(1)}, bf16[512,512]{1,0:T(8,128)(2,1)S(1)}, u32[]{:S(2)}, u32[]{:S(2)}) collective-permute-start(bf16[512,512]{1,0:T(8,128)(2,1)S(1)} %collective-permute-done.10.refs_1_), channel_id=1, source_target_pairs={{0,7},{1,0},{2,1},{3,2},{4,3},{5,4},{6,5},{7,6},{8,15},{9,8},{10,9... | collective-permute-start | bytes 1572872 | tf_op jit(solution)/shard_map/ppermute | solution.py:24
  54.0 5.1 %collective-permute-start.17 = (f32[2,128,128]{2,1,0:T(8,128)S(1)}, f32[2,128,128]{2,1,0:T(8,128)S(1)}, u32[]{:S(2)}, u32[]{:S(2)}) collective-permute-start(f32[2,128,128]{2,1,0:T(8,128)S(1)} %shard_map.85), channel_id=1, source_target_pairs={{0,48},{16,0},{32,16},{48,32},{1,49},{17,1},{33,17},{49,33},{2,50}... | collective-permute-start | bytes 393224 | tf_op jit(solution)/shard_map/ppermute | solution.py:24
  56.5 23.1 %collective-permute-start.5 = (bf16[512,512]{1,0:T(8,128)(2,1)S(1)}, bf16[512,512]{1,0:T(8,128)(2,1)S(1)}, u32[]{:S(2)}, u32[]{:S(2)}) collective-permute-start(bf16[512,512]{1,0:T(8,128)(2,1)S(1)} %collective-permute-done.4.refs_1_), channel_id=1, source_target_pairs={{0,7},{1,0},{2,1},{3,2},{4,3},{5,4},{6,5},{7,6},{8,15},{9,8},{10,9... | collective-permute-start | bytes 1572872 | tf_op jit(solution)/shard_map/ppermute | solution.py:24
  59.0 8.9 %collective-permute-start.16 = (f32[2,128,128]{2,1,0:T(8,128)S(1)}, f32[2,128,128]{2,1,0:T(8,128)S(1)}, u32[]{:S(2)}, u32[]{:S(2)}) collective-permute-start(f32[2,128,128]{2,1,0:T(8,128)S(1)} %shard_map.85), channel_id=1, source_target_pairs={{0,32},{16,48},{32,0},{48,16},{1,33},{17,49},{33,1},{49,17},{2,34}... | collective-permute-start | bytes 393224 | tf_op jit(solution)/shard_map/ppermute | solution.py:24
  61.5 19.4 %collective-permute-start.8 = (bf16[512,512]{1,0:T(8,128)(2,1)S(1)}, bf16[512,512]{1,0:T(8,128)(2,1)S(1)}, u32[]{:S(2)}, u32[]{:S(2)}) collective-permute-start(bf16[512,512]{1,0:T(8,128)(2,1)S(1)} %collective-permute-done.7.refs_0_), channel_id=1, source_target_pairs={{0,1},{1,2},{2,3},{3,4},{4,5},{5,6},{6,7},{7,0},{8,9},{9,10},{10,1... | collective-permute-start | bytes 1572872 | tf_op jit(solution)/shard_map/ppermute | solution.py:24
  65.2 22.0 %collective-permute-start.12 = (bf16[512,512]{1,0:T(8,128)(2,1)S(1)}, bf16[512,512]{1,0:T(8,128)(2,1)S(1)}, u32[]{:S(2)}, u32[]{:S(2)}) collective-permute-start(bf16[512,512]{1,0:T(8,128)(2,1)S(1)} %collective-permute-done.2.refs_0_), channel_id=1, source_target_pairs={{0,1},{1,2},{2,3},{3,4},{4,5},{5,6},{6,7},{7,0},{8,9},{9,10},{10,1... | collective-permute-start | bytes 1572872 | tf_op jit(solution)/shard_map/ppermute | solution.py:24
  65.2 22.0 %collective-permute-start.13 = (bf16[512,512]{1,0:T(8,128)(2,1)S(1)}, bf16[512,512]{1,0:T(8,128)(2,1)S(1)}, u32[]{:S(2)}, u32[]{:S(2)}) collective-permute-start(bf16[512,512]{1,0:T(8,128)(2,1)S(1)} %collective-permute-done.11.refs_1_), channel_id=1, source_target_pairs={{0,7},{1,0},{2,1},{3,2},{4,3},{5,4},{6,5},{7,6},{8,15},{9,8},{10,9... | collective-permute-start | bytes 1572872 | tf_op jit(solution)/shard_map/ppermute | solution.py:24
  67.9 5.3 %collective-permute-start.15 = (f32[2,128,128]{2,1,0:T(8,128)S(1)}, f32[2,128,128]{2,1,0:T(8,128)S(1)}, u32[]{:S(2)}, u32[]{:S(2)}) collective-permute-start(f32[2,128,128]{2,1,0:T(8,128)S(1)} %shard_map.85), channel_id=1, source_target_pairs={{0,16},{16,32},{32,48},{48,0},{1,17},{17,33},{33,49},{49,1},{2,18}... | collective-permute-start | bytes 393224 | tf_op jit(solution)/shard_map/ppermute | solution.py:24
  73.3 21.5 %collective-permute-start.20 = (f32[2,128,128]{2,1,0:T(8,128)S(1)}, f32[2,128,128]{2,1,0:T(8,128)S(1)}, u32[]{:S(2)}, u32[]{:S(2)}) collective-permute-start(f32[2,128,128]{2,1,0:T(8,128)S(1)} %get-tuple-element.41), channel_id=1, source_target_pairs={{0,192},{64,0},{128,64},{192,128},{1,193},{65,1},{129,65},{193,129... | collective-permute-start | bytes 393224 | tf_op jit(solution)/shard_map/ppermute | solution.py:24
  79.6 15.7 %collective-permute-start.19 = (f32[2,128,128]{2,1,0:T(8,128)S(1)}, f32[2,128,128]{2,1,0:T(8,128)S(1)}, u32[]{:S(2)}, u32[]{:S(2)}) collective-permute-start(f32[2,128,128]{2,1,0:T(8,128)S(1)} %get-tuple-element.41), channel_id=1, source_target_pairs={{0,128},{64,192},{128,0},{192,64},{1,129},{65,193},{129,1},{193,65... | collective-permute-start | bytes 393224 | tf_op jit(solution)/shard_map/ppermute | solution.py:24
  80.8 14.5 %collective-permute-start.18 = (f32[2,128,128]{2,1,0:T(8,128)S(1)}, f32[2,128,128]{2,1,0:T(8,128)S(1)}, u32[]{:S(2)}, u32[]{:S(2)}) collective-permute-start(f32[2,128,128]{2,1,0:T(8,128)S(1)} %get-tuple-element.41), channel_id=1, source_target_pairs={{0,64},{64,128},{128,192},{192,0},{1,65},{65,129},{129,193},{193,1... | collective-permute-start | bytes 393224 | tf_op jit(solution)/shard_map/ppermute | solution.py:24
  91.7 5.3 %collective-permute-start.25 = (bf16[2,128,128]{2,1,0:T(8,128)(2,1)S(1)}, bf16[2,128,128]{2,1,0:T(8,128)(2,1)S(1)}, u32[]{:S(2)}, u32[]{:S(2)}) collective-permute-start(bf16[2,128,128]{2,1,0:T(8,128)(2,1)S(1)} %shard_map.92), channel_id=1, source_target_pairs={{0,48},{16,0},{32,16},{48,32},{1,49},{17,1},{33,17},{49,33},{2,50}... | collective-permute-start | bytes 196616 | tf_op jit(solution)/shard_map/ppermute | solution.py:24
  94.8 5.9 %collective-permute-start.23 = (bf16[2,128,128]{2,1,0:T(8,128)(2,1)S(1)}, bf16[2,128,128]{2,1,0:T(8,128)(2,1)S(1)}, u32[]{:S(2)}, u32[]{:S(2)}) collective-permute-start(bf16[2,128,128]{2,1,0:T(8,128)(2,1)S(1)} %shard_map.92), channel_id=1, source_target_pairs={{0,16},{16,32},{32,48},{48,0},{1,17},{17,33},{33,49},{49,1},{2,18}... | collective-permute-start | bytes 196616 | tf_op jit(solution)/shard_map/ppermute | solution.py:24
  95.4 9.1 %collective-permute-start.21 = (bf16[2,128,128]{2,1,0:T(8,128)(2,1)S(1)}, bf16[2,128,128]{2,1,0:T(8,128)(2,1)S(1)}, u32[]{:S(2)}, u32[]{:S(2)}) collective-permute-start(bf16[2,128,128]{2,1,0:T(8,128)(2,1)S(1)} %get-tuple-element.43), channel_id=1, source_target_pairs={{0,8},{8,0},{1,9},{9,1},{2,10},{10,2},{3,11},{11,3},{4,12},{12,4},... | collective-permute-start | bytes 196616 | tf_op jit(solution)/shard_map/ppermute | solution.py:24
  108.9 5.9 %collective-permute-start.29 = (bf16[2,128,128]{2,1,0:T(8,128)(2,1)S(1)}, bf16[2,128,128]{2,1,0:T(8,128)(2,1)S(1)}, u32[]{:S(2)}, u32[]{:S(2)}) collective-permute-start(bf16[2,128,128]{2,1,0:T(8,128)(2,1)S(1)} %get-tuple-element.62), channel_id=1, source_target_pairs={{0,8},{8,0},{1,9},{9,1},{2,10},{10,2},{3,11},{11,3},{4,12},{12,4},... | collective-permute-start | bytes 196616 | tf_op jit(solution)/shard_map/ppermute | solution.py:24
  (12 other events, 133.5 us)
